TPU v7x, 32 devices: a whole 2x2x4 slice. The times are simulated.
32 devices in a mesh: tile: 8 (over y, x, core), depth: 4 (over z).
Axes of the slice: x: 2, y: 2, z: 4, core: 2. Of those that a mesh axis runs over, the one named last changes fastest.
Arguments:
- initial_state: float32 [2, 32, 8192], P(None, 'depth', 'tile'), may hold values from -6 to 6
- observed: float32 [2, 32, 8192], P(None, 'depth', 'tile'), may hold values from -6 to 6
- edge_weight: float32 [8192], P('tile'), may hold values from 0.25 to 1
- land: int32 [8192], P('tile'), may hold values 0 or 1
- w_in: bfloat16 [64, 640], replicated, may hold values from -0.75 to 0.75
- b_in: float32 [640], replicated, may hold values from -3 to 3
- w_mid: bfloat16 [640, 640], replicated, may hold values from -0.25 to 0.25
- b_mid: float32 [640], replicated, may hold values from -3 to 3
- w_out: bfloat16 [640, 64], replicated, may hold values from -0.25 to 0.25
- b_out: float32 [64], replicated, may hold values from -3 to 3
Outputs:
- final_state: float32 [2, 32, 8192], P(None, 'depth', 'tile')
- sensitivity: float32 [2, 32, 8192], P(None, 'depth', 'tile')
- grad_w_in: float32 [64, 640], replicated
- grad_b_in: float32 [640], replicated
- grad_w_mid: float32 [640, 640], replicated
- grad_b_mid: float32 [640], replicated
- grad_w_out: float32 [640, 64], replicated
- grad_b_out: float32 [64], replicated
All inputs are finite; a program needn't handle non-finite values. No bound on the sum of `land` on one device may be relied on, other than what follows from the above.
Results may differ from a plain program's by a relative error of at most 0.0017.
Values may be sent and summed in bfloat16 or wider, within the bound.
No kernel may reach another device: no remote copies, remote signals or barrier semaphores. Data moves between devices by JAX's collectives and lax.ppermute only.
A program may use at most 64 MiB of HBM per device.

v0:
```python
import jax
import jax.numpy as jnp
from jax import lax
from jax.sharding import PartitionSpec as P

TILE_SIDE = 32
LEVELS = 32
TIME_STEPS = 2
FEATURES = 64
TILE_CELLS = 1024
diffuse_coef = 0.2
step_size = 0.5


def with_halo(cells, sides, width):
    for axis, dim in sides:
        count = lax.axis_size(axis)
        head = lax.slice_in_dim(cells, 0, width, axis=dim)
        tail = lax.slice_in_dim(cells, cells.shape[dim] - width, cells.shape[dim], axis=dim)
        cells = jnp.concatenate(
            [
                lax.ppermute(tail, axis, [(i, (i + 1) % count) for i in range(count)]),
                cells,
                lax.ppermute(head, axis, [((i + 1) % count, i) for i in range(count)]),
            ],
            axis=dim,
        )
    return cells


def passed_along(x, axis, by):
    length = lax.axis_size(axis)
    return lax.ppermute(x, axis, [(i, (i + by) % length) for i in range(length)])


def neighbour_sum(flat_rows):
    row_count = flat_rows.shape[0]
    tile_grid = flat_rows.reshape(row_count, TILE_SIDE, TILE_SIDE)
    zonal_pair = jnp.stack([tile_grid[:, :, -1], tile_grid[:, :, 0]], axis=1)
    padded = with_halo(zonal_pair[None], (("tile", 0),), 1)
    from_west = padded[0, :, 0, :]
    from_east = padded[2, :, 1, :]
    fold_pair = jnp.stack([tile_grid[:, 0, :], tile_grid[:, -1, :]], axis=1)
    across = passed_along(fold_pair, "tile", lax.axis_size("tile") // 2)[:, :, ::-1]
    west_cells = jnp.concatenate([from_west[:, :, None], tile_grid[:, :, :-1]], axis=2)
    east_cells = jnp.concatenate([tile_grid[:, :, 1:], from_east[:, :, None]], axis=2)
    south_cells = jnp.concatenate([across[:, 0, None, :], tile_grid[:, :-1, :]], axis=1)
    north_cells = jnp.concatenate([tile_grid[:, 1:, :], across[:, 1, None, :]], axis=1)
    return (west_cells + east_cells + south_cells + north_cells).reshape(row_count, TILE_CELLS)


def diffuse(tracer_field, weight, weight_sums):
    flat_rows = tracer_field.reshape(-1, TILE_CELLS)
    scaled = flat_rows * weight[None, :]
    result_rows = weight[None, :] * (neighbour_sum(scaled) - flat_rows * weight_sums[None, :])
    return result_rows.reshape(tracer_field.shape)


def silu_slope(pre_act):
    sigmoid_val = jax.nn.sigmoid(pre_act)
    return sigmoid_val * (1.0 + pre_act * (1.0 - sigmoid_val))


def closure_forward(inputs, params):
    w_in, b_in, w_mid, b_mid, w_out, b_out = params
    contract_rows = (((0,), (0,)), ((), ()))
    pre_one = (
        lax.dot_general(w_in, inputs, contract_rows, preferred_element_type=jnp.float32)
        + b_in[:, None]
    )
    hidden_one = jax.nn.silu(pre_one).astype(jnp.bfloat16)
    pre_two = (
        lax.dot_general(w_mid, hidden_one, contract_rows, preferred_element_type=jnp.float32)
        + b_mid[:, None]
    )
    hidden_two = jax.nn.silu(pre_two).astype(jnp.bfloat16)
    output = (
        lax.dot_general(w_out, hidden_two, contract_rows, preferred_element_type=jnp.float32)
        + b_out[:, None]
    )
    return (output, (inputs, pre_one, hidden_one, pre_two, hidden_two))


def closure_backward(upstream, saved_cache, params):
    w_in, b_in, w_mid, b_mid, w_out, b_out = params
    inputs, pre_one, hidden_one, pre_two, hidden_two = saved_cache
    contract_cols = (((1,), (1,)), ((), ()))
    grad_w_out = lax.dot_general(
        hidden_two, upstream, contract_cols, preferred_element_type=jnp.float32
    )
    grad_b_out = jnp.sum(upstream.astype(jnp.float32), axis=1)
    slope_two = (
        jnp.dot(w_out, upstream, preferred_element_type=jnp.float32) * silu_slope(pre_two)
    ).astype(jnp.bfloat16)
    grad_w_mid = lax.dot_general(
        hidden_one, slope_two, contract_cols, preferred_element_type=jnp.float32
    )
    grad_b_mid = jnp.sum(slope_two.astype(jnp.float32), axis=1)
    slope_one = (
        jnp.dot(w_mid, slope_two, preferred_element_type=jnp.float32) * silu_slope(pre_one)
    ).astype(jnp.bfloat16)
    grad_w_in = lax.dot_general(
        inputs, slope_one, contract_cols, preferred_element_type=jnp.float32
    )
    grad_b_in = jnp.sum(slope_one.astype(jnp.float32), axis=1)
    back_grad = jnp.dot(w_in, slope_one, preferred_element_type=jnp.float32)
    return (back_grad, (grad_w_in, grad_b_in, grad_w_mid, grad_b_mid, grad_w_out, grad_b_out))


def body(initial_state, observed, edge_weight, land, w_in, b_in, w_mid, b_mid, w_out, b_out):
    params = (w_in, b_in, w_mid, b_mid, w_out, b_out)
    ocean_mask = land.astype(jnp.float32)
    weight = edge_weight * ocean_mask
    weight_sums = neighbour_sum(weight[None, :])[0]

    def to_columns(segment):
        full_cols = lax.all_to_all(segment, "depth", split_axis=2, concat_axis=1, tiled=True)
        return full_cols.reshape(FEATURES, full_cols.shape[2])

    def to_segments(values):
        shaped = values.reshape(2, LEVELS, values.shape[1])
        segment_part = lax.all_to_all(shaped, "depth", split_axis=1, concat_axis=2, tiled=True)
        return segment_part

    state_now = initial_state
    caches = []
    for step_index in range(TIME_STEPS):
        inputs = to_columns(state_now.astype(jnp.bfloat16))
        tendency, saved_cache = closure_forward(inputs, params)
        caches.append(saved_cache)
        change = diffuse(state_now, weight, weight_sums)
        state_now = (
            state_now
            + diffuse_coef * change
            + step_size * ocean_mask[None, None, :] * to_segments(tendency)
        )
    adjoint = ocean_mask[None, None, :] * (state_now - observed)
    grad_list = []
    for step_index in reversed(range(TIME_STEPS)):
        upstream = to_columns(
            (step_size * ocean_mask[None, None, :] * adjoint).astype(jnp.bfloat16)
        )
        back_grad, param_grads = closure_backward(upstream, caches[step_index], params)
        grad_list.append(param_grads)
        spread = diffuse(adjoint, weight, weight_sums)
        adjoint = adjoint + diffuse_coef * spread + to_segments(back_grad)
    totals = grad_list[0]
    for param_grads in grad_list[1:]:
        totals = tuple((total + gradient for total, gradient in zip(totals, param_grads)))
    summed = lax.psum(totals, ("tile", "depth"))
    grad_scale = 1.0 / (lax.axis_size("tile") * TILE_CELLS)
    return (
        state_now,
        adjoint,
        summed[0] * grad_scale,
        summed[1] * grad_scale,
        summed[2] * grad_scale,
        summed[3] * grad_scale,
        summed[4] * grad_scale,
        summed[5] * grad_scale,
    )


def solution(mesh):
    return jax.shard_map(
        body,
        mesh=mesh,
        in_specs=(
            P(None, "depth", "tile"),
            P(None, "depth", "tile"),
            P("tile"),
            P("tile"),
            P(),
            P(),
            P(),
            P(),
            P(),
            P(),
        ),
        out_specs=(
            P(None, "depth", "tile"),
            P(None, "depth", "tile"),
            P(),
            P(),
            P(),
            P(),
            P(),
            P(),
        ),
        check_vma=False,
    )
```

profile of v0, /device:TPU:0, one launch (start us, length us, event | category | flops | bytes accessed | tf_op | source)
XLA Modules:
  0.0 276.7 jit_solution(8364587519596231876)
XLA Ops:
  8.2 3.4 %collective-permute-start.4 = (f32[1,1,2,32]{3,2,1,0:T(2,128)S(1)}, f32[1,1,2,32]{3,2,1,0:T(2,128)S(1)}, u32[]{:S(2)}, u32[]{:S(2)}) collective-permute-start(f32[1,1,2,32]{3,2,1,0:T(2,128)S(1)} %maximum_bitcast_fusion.4), channel_id=1, source_target_pairs={{4,0},{8,4},{12,8},{16,12},{20,16},{24,20},{28,24},{0,28},{5,1},{9... | collective-permute-start | bytes 776 | tf_op jit(solution)/shard_map/ppermute | solution.py:24
  13.0 2.7 collective-permute-start.1
  18.7 4.9 %all-to-all-start = ((bf16[4,2,2048]{2,1,0:T(2,128)(2,1)}), bf16[4,2,2048]{2,1,0:T(2,128)(2,1)S(1)}, u32[]{:S(2)}, u32[]{:S(2)}) async-start(bf16[4,2,2048]{2,1,0:T(2,128)(2,1)} %reshape.252), calls=%async_computation | async-start | bytes 65536 | tf_op jit(solution)/shard_map/all_to_all | solution.py:117
  25.2 1.5 collective-permute-start.2
  27.2 1.7 collective-permute-done.2
  35.0 5.1 %all-to-all-start.1 = ((f32[2,32,256]{2,0,1:T(2,128)}), f32[2,32,256]{2,0,1:T(2,128)}, u32[]{:S(2)}, u32[]{:S(2)}) async-start(f32[2,32,256]{2,0,1:T(2,128)} %copy.161), calls=%async_computation.1 | async-start | bytes 131072 | tf_op jit(solution)/shard_map/all_to_all | solution.py:122
  41.3 4.5 %all-to-all-done.1 = f32[2,32,256]{2,0,1:T(2,128)} async-done(((f32[2,32,256]{2,0,1:T(2,128)}), f32[2,32,256]{2,0,1:T(2,128)}, u32[]{:S(2)}, u32[]{:S(2)}) %all-to-all-start.1) | async-done | bytes 65568 | tf_op jit(solution)/shard_map/all_to_all | solution.py:122
  48.7 1.6 collective-permute-start.8
  52.6 3.3 %all-to-all-start.2 = ((bf16[4,2,2048]{2,1,0:T(2,128)(2,1)}), bf16[4,2,2048]{2,1,0:T(2,128)(2,1)S(1)}, u32[]{:S(2)}, u32[]{:S(2)}) async-start(bf16[4,2,2048]{2,1,0:T(2,128)(2,1)} %reshape.254), calls=%async_computation.2 | async-start | bytes 65536 | tf_op jit(solution)/shard_map/all_to_all | solution.py:117
  57.7 3.8 %all-to-all-done.2 = bf16[4,2,2048]{2,1,0:T(2,128)(2,1)S(1)} async-done(((bf16[4,2,2048]{2,1,0:T(2,128)(2,1)}), bf16[4,2,2048]{2,1,0:T(2,128)(2,1)S(1)}, u32[]{:S(2)}, u32[]{:S(2)}) %all-to-all-start.2) | async-done | bytes 32800 | tf_op jit(solution)/shard_map/all_to_all | solution.py:117
  63.4 2.3 multiply_convert_fusion
  66.6 3.9 %all-to-all-start.3 = ((f32[2,32,256]{2,0,1:T(2,128)}), f32[2,32,256]{2,0,1:T(2,128)}, u32[]{:S(2)}, u32[]{:S(2)}) async-start(f32[2,32,256]{2,0,1:T(2,128)} %copy.168), calls=%async_computation.3 | async-start | bytes 131072 | tf_op jit(solution)/shard_map/all_to_all | solution.py:122
  72.0 4.4 %all-to-all-done.3 = f32[2,32,256]{2,0,1:T(2,128)} async-done(((f32[2,32,256]{2,0,1:T(2,128)}), f32[2,32,256]{2,0,1:T(2,128)}, u32[]{:S(2)}, u32[]{:S(2)}) %all-to-all-start.3) | async-done | bytes 65568 | tf_op jit(solution)/shard_map/all_to_all | solution.py:122
  77.2 1.5 multiply_convert_fusion.5
  82.9 4.0 %all-to-all-start.4 = ((bf16[4,2,2048]{2,1,0:T(2,128)(2,1)}), bf16[4,2,2048]{2,1,0:T(2,128)(2,1)}, u32[]{:S(2)}, u32[]{:S(2)}) async-start(bf16[4,2,2048]{2,1,0:T(2,128)(2,1)} %reshape.256), calls=%async_computation.4 | async-start | bytes 65536 | tf_op jit(solution)/shard_map/all_to_all | solution.py:117
  90.2 2.3 all-to-all-done.4
  95.1 1.5 convert_reduce_fusion.1
  97.7 1.7 fusion.22
  100.3 3.3 %all-to-all-start.5 = ((f32[2,32,256]{2,0,1:T(2,128)}), f32[2,32,256]{2,0,1:T(2,128)S(1)}, u32[]{:S(2)}, u32[]{:S(2)}) async-start(f32[2,32,256]{2,0,1:T(2,128)} %copy.175), calls=%async_computation.5 | async-start | bytes 131072 | tf_op jit(solution)/shard_map/all_to_all | solution.py:122
  104.5 4.8 %all-to-all-done.5 = f32[2,32,256]{2,0,1:T(2,128)S(1)} async-done(((f32[2,32,256]{2,0,1:T(2,128)}), f32[2,32,256]{2,0,1:T(2,128)S(1)}, u32[]{:S(2)}, u32[]{:S(2)}) %all-to-all-start.5) | async-done | bytes 65568 | tf_op jit(solution)/shard_map/all_to_all | solution.py:122
  110.6 1.6 collective-permute-start.14
  114.4 3.9 %all-to-all-start.6 = ((bf16[4,2,2048]{2,1,0:T(2,128)(2,1)}), bf16[4,2,2048]{2,1,0:T(2,128)(2,1)}, u32[]{:S(2)}, u32[]{:S(2)}) async-start(bf16[4,2,2048]{2,1,0:T(2,128)(2,1)} %reshape.258), calls=%async_computation.6 | async-start | bytes 65536 | tf_op jit(solution)/shard_map/all_to_all | solution.py:117
  120.3 3.7 %all-to-all-done.6 = bf16[4,2,2048]{2,1,0:T(2,128)(2,1)} async-done(((bf16[4,2,2048]{2,1,0:T(2,128)(2,1)}), bf16[4,2,2048]{2,1,0:T(2,128)(2,1)}, u32[]{:S(2)}, u32[]{:S(2)}) %all-to-all-start.6) | async-done | bytes 32800 | tf_op jit(solution)/shard_map/all_to_all | solution.py:117
  125.8 1.8 convolution_add_fusion.5
  127.6 1.5 convert_reduce_fusion
  130.8 1.7 convolution_add_fusion
  134.3 3.3 %all-to-all-start.7 = ((f32[2,32,256]{2,0,1:T(2,128)}), f32[2,32,256]{2,0,1:T(2,128)S(1)}, u32[]{:S(2)}, u32[]{:S(2)}) async-start(f32[2,32,256]{2,0,1:T(2,128)} %copy.182), calls=%async_computation.7 | async-start | bytes 131072 | tf_op jit(solution)/shard_map/all_to_all | solution.py:122
  137.6 40.0 %all-reduce = (f32[640]{0:T(1024)S(1)}, f32[640]{0:T(1024)S(1)}, f32[64]{0:T(128)S(1)}) all-reduce(f32[640]{0:T(1024)S(1)} %add.309, f32[640]{0:T(1024)S(1)} %add.311, f32[64]{0:T(128)S(1)} %add.314), channel_id=1, replica_groups=mesh['tile'=8,'depth'=4] {'tile','depth'}, use_global_device_ids=true, to_apply=%region_3.4 | all-reduce | flops 1344 | bytes 10752 | tf_op jit(solution)/shard_map/psum | solution.py:150
  180.0 84.0 %all-reduce.4.cloned.1.call-done = (f32[64,640]{1,0:T(8,128)}, f32[640,640]{1,0:T(8,128)}, f32[640,64]{0,1:T(8,128)}) async-done(((f32[64,640]{1,0:T(8,128)}, f32[640,640]{1,0:T(8,128)}, f32[640,64]{0,1:T(8,128)}), (f32[64,640]{1,0:T(8,128)}, f32[640,640]{1,0:T(8,128)}, f32[640,64]{0,1:T(8,128)})) %all-reduce.4.cloned.1.call-update) | async-done | bytes 1966096 | tf_op jit(solution)/shard_map/psum | solution.py:150
  264.0 1.6 broadcast_multiply_fusion.6
  265.6 1.6 broadcast_multiply_fusion.5
  267.2 2.7 broadcast_multiply_fusion
  (224 shorter events, 52.3 us)
Async XLA Ops:
  7.2 25.5 %copy-start = (bf16[640,640]{1,0:T(8,128)(2,1)S(1)}, bf16[640,640]{1,0:T(8,128)(2,1)}, u32[]{:S(2)}) copy-start(bf16[640,640]{1,0:T(8,128)(2,1)} %param.16) | copy-start | bytes 2457604
  8.2 18.7 %collective-permute-start.4 = (f32[1,1,2,32]{3,2,1,0:T(2,128)S(1)}, f32[1,1,2,32]{3,2,1,0:T(2,128)S(1)}, u32[]{:S(2)}, u32[]{:S(2)}) collective-permute-start(f32[1,1,2,32]{3,2,1,0:T(2,128)S(1)} %maximum_bitcast_fusion.4), channel_id=1, source_target_pairs={{4,0},{8,4},{12,8},{16,12},{20,16},{24,20},{28,24},{0,28},{5,1},{9... | collective-permute-start | bytes 776 | tf_op jit(solution)/shard_map/ppermute | solution.py:24
  11.6 13.5 %collective-permute-start.3 = (f32[1,1,2,32]{3,2,1,0:T(2,128)S(1)}, f32[1,1,2,32]{3,2,1,0:T(2,128)S(1)}, u32[]{:S(2)}, u32[]{:S(2)}) collective-permute-start(f32[1,1,2,32]{3,2,1,0:T(2,128)S(1)} %maximum_bitcast_fusion.4), channel_id=1, source_target_pairs={{0,4},{4,8},{8,12},{12,16},{16,20},{20,24},{24,28},{28,0},{1,5},{5... | collective-permute-start | bytes 776 | tf_op jit(solution)/shard_map/ppermute | solution.py:22
  13.0 15.9 %collective-permute-start.1 = (f32[1,16,2,32]{3,1,2,0:T(8,128)S(1)}, f32[1,16,2,32]{3,1,2,0:T(8,128)S(1)}, u32[]{:S(2)}, u32[]{:S(2)}) collective-permute-start(f32[1,16,2,32]{3,1,2,0:T(8,128)S(1)} %maximum_bitcast_fusion), channel_id=1, source_target_pairs={{4,0},{8,4},{12,8},{16,12},{20,16},{24,20},{28,24},{0,28},{5,1},{9... | collective-permute-start | bytes 12296 | tf_op jit(solution)/shard_map/ppermute | solution.py:24
  15.7 13.2 %collective-permute-start = (f32[1,16,2,32]{3,1,2,0:T(8,128)S(1)}, f32[1,16,2,32]{3,1,2,0:T(8,128)S(1)}, u32[]{:S(2)}, u32[]{:S(2)}) collective-permute-start(f32[1,16,2,32]{3,1,2,0:T(8,128)S(1)} %maximum_bitcast_fusion), channel_id=1, source_target_pairs={{0,4},{4,8},{8,12},{12,16},{16,20},{20,24},{24,28},{28,0},{1,5},{5... | collective-permute-start | bytes 12296 | tf_op jit(solution)/shard_map/ppermute | solution.py:22
  15.7 10.9 %collective-permute-start.5 = (f32[1,2,32]{2,1,0:T(2,128)S(1)}, f32[1,2,32]{2,1,0:T(2,128)S(1)}, u32[]{:S(2)}, u32[]{:S(2)}) collective-permute-start(f32[1,2,32]{2,1,0:T(2,128)S(1)} %pad_maximum_fusion.4), channel_id=1, source_target_pairs={{0,16},{4,20},{8,24},{12,28},{16,0},{20,4},{24,8},{28,12},{1,17},{... | collective-permute-start | bytes 776 | tf_op jit(solution)/shard_map/ppermute | solution.py:33
  17.2 7.4 %copy-start.23 = (s32[1024]{0:T(1024)S(1)}, s32[1024]{0:T(1024)}, u32[]{:S(2)}) copy-start(s32[1024]{0:T(1024)} %param.13) | copy-start | bytes 12292
  18.7 12.1 %all-to-all-start = ((bf16[4,2,2048]{2,1,0:T(2,128)(2,1)}), bf16[4,2,2048]{2,1,0:T(2,128)(2,1)S(1)}, u32[]{:S(2)}, u32[]{:S(2)}) async-start(bf16[4,2,2048]{2,1,0:T(2,128)(2,1)} %reshape.252), calls=%async_computation | async-start | bytes 65536 | tf_op jit(solution)/shard_map/all_to_all | solution.py:117
  23.8 8.6 %copy-start.2 = (bf16[64,640]{1,0:T(8,128)(2,1)S(1)}, bf16[64,640]{1,0:T(8,128)(2,1)}, u32[]{:S(2)}) copy-start(bf16[64,640]{1,0:T(8,128)(2,1)} %param.14) | copy-start | bytes 245764
  23.8 8.6 %copy-start.21 = (f32[640]{0:T(1024)S(1)}, f32[640]{0:T(1024)}, u32[]{:S(2)}) copy-start(f32[640]{0:T(1024)} %param.15) | copy-start | bytes 7684
  24.5 8.1 %copy-start.27 = (f32[640]{0:T(1024)S(1)}, f32[640]{0:T(1024)}, u32[]{:S(2)}) copy-start(f32[640]{0:T(1024)} %param.17) | copy-start | bytes 7684
  25.2 3.7 %collective-permute-start.2 = (f32[16,2,32]{2,1,0:T(2,128)S(1)}, f32[16,2,32]{2,1,0:T(2,128)S(1)}, u32[]{:S(2)}, u32[]{:S(2)}) collective-permute-start(f32[16,2,32]{2,1,0:T(2,128)S(1)} %pad_maximum_fusion), channel_id=1, source_target_pairs={{0,16},{4,20},{8,24},{12,28},{16,0},{20,4},{24,8},{28,12},{1,17},{... | collective-permute-start | bytes 12296 | tf_op jit(solution)/shard_map/ppermute | solution.py:33
  34.0 12.7 %copy-start.10 = (f32[2,8,1024]{2,1,0:T(8,128)S(1)}, f32[2,8,1024]{2,1,0:T(8,128)}, u32[]{:S(2)}) copy-start(f32[2,8,1024]{2,1,0:T(8,128)} %param.10) | copy-start | bytes 196612
  35.0 10.9 %all-to-all-start.1 = ((f32[2,32,256]{2,0,1:T(2,128)}), f32[2,32,256]{2,0,1:T(2,128)}, u32[]{:S(2)}, u32[]{:S(2)}) async-start(f32[2,32,256]{2,0,1:T(2,128)} %copy.161), calls=%async_computation.1 | async-start | bytes 131072 | tf_op jit(solution)/shard_map/all_to_all | solution.py:122
  47.3 8.6 %collective-permute-start.7 = (f32[1,16,2,32]{3,1,2,0:T(8,128)S(1)}, f32[1,16,2,32]{3,1,2,0:T(8,128)S(1)}, u32[]{:S(2)}, u32[]{:S(2)}) collective-permute-start(f32[1,16,2,32]{3,1,2,0:T(8,128)S(1)} %maximum_bitcast_fusion.1), channel_id=1, source_target_pairs={{4,0},{8,4},{12,8},{16,12},{20,16},{24,20},{28,24},{0,28},{5,1},{9... | collective-permute-start | bytes 12296 | tf_op jit(solution)/shard_map/ppermute | solution.py:24
  47.4 8.6 %collective-permute-start.6 = (f32[1,16,2,32]{3,1,2,0:T(8,128)S(1)}, f32[1,16,2,32]{3,1,2,0:T(8,128)S(1)}, u32[]{:S(2)}, u32[]{:S(2)}) collective-permute-start(f32[1,16,2,32]{3,1,2,0:T(8,128)S(1)} %maximum_bitcast_fusion.1), channel_id=1, source_target_pairs={{0,4},{4,8},{8,12},{12,16},{16,20},{20,24},{24,28},{28,0},{1,5},{5... | collective-permute-start | bytes 12296 | tf_op jit(solution)/shard_map/ppermute | solution.py:22
  48.7 7.2 %collective-permute-start.8 = (f32[16,2,32]{2,1,0:T(2,128)S(1)}, f32[16,2,32]{2,1,0:T(2,128)S(1)}, u32[]{:S(2)}, u32[]{:S(2)}) collective-permute-start(f32[16,2,32]{2,1,0:T(2,128)S(1)} %pad_maximum_fusion.1), channel_id=1, source_target_pairs={{0,16},{4,20},{8,24},{12,28},{16,0},{20,4},{24,8},{28,12},{1,17},{... | collective-permute-start | bytes 12296 | tf_op jit(solution)/shard_map/ppermute | solution.py:33
  52.6 8.9 %all-to-all-start.2 = ((bf16[4,2,2048]{2,1,0:T(2,128)(2,1)}), bf16[4,2,2048]{2,1,0:T(2,128)(2,1)S(1)}, u32[]{:S(2)}, u32[]{:S(2)}) async-start(bf16[4,2,2048]{2,1,0:T(2,128)(2,1)} %reshape.254), calls=%async_computation.2 | async-start | bytes 65536 | tf_op jit(solution)/shard_map/all_to_all | solution.py:117
  65.7 11.5 %copy-start.22 = (f32[1024]{0:T(1024)S(1)}, f32[1024]{0:T(1024)}, u32[]{:S(2)}) copy-start(f32[1024]{0:T(1024)} %convert_element_type.59) | copy-start | bytes 12292
  66.6 9.7 %all-to-all-start.3 = ((f32[2,32,256]{2,0,1:T(2,128)}), f32[2,32,256]{2,0,1:T(2,128)}, u32[]{:S(2)}, u32[]{:S(2)}) async-start(f32[2,32,256]{2,0,1:T(2,128)} %copy.168), calls=%async_computation.3 | async-start | bytes 131072 | tf_op jit(solution)/shard_map/all_to_all | solution.py:122
  79.2 9.4 %collective-permute-start.10 = (f32[1,16,2,32]{3,1,2,0:T(8,128)S(1)}, f32[1,16,2,32]{3,1,2,0:T(8,128)S(1)}, u32[]{:S(2)}, u32[]{:S(2)}) collective-permute-start(f32[1,16,2,32]{3,1,2,0:T(8,128)S(1)} %maximum_bitcast_fusion.2), channel_id=1, source_target_pairs={{4,0},{8,4},{12,8},{16,12},{20,16},{24,20},{28,24},{0,28},{5,1},{9... | collective-permute-start | bytes 12296 | tf_op jit(solution)/shard_map/ppermute | solution.py:24
  79.3 7.6 %collective-permute-start.9 = (f32[1,16,2,32]{3,1,2,0:T(8,128)S(1)}, f32[1,16,2,32]{3,1,2,0:T(8,128)S(1)}, u32[]{:S(2)}, u32[]{:S(2)}) collective-permute-start(f32[1,16,2,32]{3,1,2,0:T(8,128)S(1)} %maximum_bitcast_fusion.2), channel_id=1, source_target_pairs={{0,4},{4,8},{8,12},{12,16},{16,20},{20,24},{24,28},{28,0},{1,5},{5... | collective-permute-start | bytes 12296 | tf_op jit(solution)/shard_map/ppermute | solution.py:22
  80.0 7.0 %collective-permute-start.11 = (f32[16,2,32]{2,1,0:T(2,128)S(1)}, f32[16,2,32]{2,1,0:T(2,128)S(1)}, u32[]{:S(2)}, u32[]{:S(2)}) collective-permute-start(f32[16,2,32]{2,1,0:T(2,128)S(1)} %pad_maximum_fusion.2), channel_id=1, source_target_pairs={{0,16},{4,20},{8,24},{12,28},{16,0},{20,4},{24,8},{28,12},{1,17},{... | collective-permute-start | bytes 12296 | tf_op jit(solution)/shard_map/ppermute | solution.py:33
  82.9 9.6 %all-to-all-start.4 = ((bf16[4,2,2048]{2,1,0:T(2,128)(2,1)}), bf16[4,2,2048]{2,1,0:T(2,128)(2,1)}, u32[]{:S(2)}, u32[]{:S(2)}) async-start(bf16[4,2,2048]{2,1,0:T(2,128)(2,1)} %reshape.256), calls=%async_computation.4 | async-start | bytes 65536 | tf_op jit(solution)/shard_map/all_to_all | solution.py:117
  97.7 11.6 %copy-start.8 = (f32[2,8,1024]{2,1,0:T(8,128)S(1)}, f32[2,8,1024]{2,1,0:T(8,128)}, u32[]{:S(2)}) copy-start(f32[2,8,1024]{2,1,0:T(8,128)} %copy-done.7) | copy-start | bytes 196612
  100.3 9.0 %all-to-all-start.5 = ((f32[2,32,256]{2,0,1:T(2,128)}), f32[2,32,256]{2,0,1:T(2,128)S(1)}, u32[]{:S(2)}, u32[]{:S(2)}) async-start(f32[2,32,256]{2,0,1:T(2,128)} %copy.175), calls=%async_computation.5 | async-start | bytes 131072 | tf_op jit(solution)/shard_map/all_to_all | solution.py:122
  109.9 8.9 %collective-permute-start.13 = (f32[1,16,2,32]{3,1,2,0:T(8,128)S(1)}, f32[1,16,2,32]{3,1,2,0:T(8,128)S(1)}, u32[]{:S(2)}, u32[]{:S(2)}) collective-permute-start(f32[1,16,2,32]{3,1,2,0:T(8,128)S(1)} %maximum_bitcast_fusion.3), channel_id=1, source_target_pairs={{4,0},{8,4},{12,8},{16,12},{20,16},{24,20},{28,24},{0,28},{5,1},{9... | collective-permute-start | bytes 12296 | tf_op jit(solution)/shard_map/ppermute | solution.py:24
  110.0 8.4 %collective-permute-start.12 = (f32[1,16,2,32]{3,1,2,0:T(8,128)S(1)}, f32[1,16,2,32]{3,1,2,0:T(8,128)S(1)}, u32[]{:S(2)}, u32[]{:S(2)}) collective-permute-start(f32[1,16,2,32]{3,1,2,0:T(8,128)S(1)} %maximum_bitcast_fusion.3), channel_id=1, source_target_pairs={{0,4},{4,8},{8,12},{12,16},{16,20},{20,24},{24,28},{28,0},{1,5},{5... | collective-permute-start | bytes 12296 | tf_op jit(solution)/shard_map/ppermute | solution.py:22
  110.6 7.7 %collective-permute-start.14 = (f32[16,2,32]{2,1,0:T(2,128)S(1)}, f32[16,2,32]{2,1,0:T(2,128)S(1)}, u32[]{:S(2)}, u32[]{:S(2)}) collective-permute-start(f32[16,2,32]{2,1,0:T(2,128)S(1)} %pad_maximum_fusion.3), channel_id=1, source_target_pairs={{0,16},{4,20},{8,24},{12,28},{16,0},{20,4},{24,8},{28,12},{1,17},{... | collective-permute-start | bytes 12296 | tf_op jit(solution)/shard_map/ppermute | solution.py:33
  114.4 9.6 %all-to-all-start.6 = ((bf16[4,2,2048]{2,1,0:T(2,128)(2,1)}), bf16[4,2,2048]{2,1,0:T(2,128)(2,1)}, u32[]{:S(2)}, u32[]{:S(2)}) async-start(bf16[4,2,2048]{2,1,0:T(2,128)(2,1)} %reshape.258), calls=%async_computation.6 | async-start | bytes 65536 | tf_op jit(solution)/shard_map/all_to_all | solution.py:117
  118.3 145.7 %all-reduce.4.cloned.1.call-start = ((), (), s32[]{:S(2)}) async-start(), calls=%async_computation.8 | async-start | bytes 3932160 | tf_op jit(solution)/shard_map/psum | solution.py:150
  134.3 45.1 %all-to-all-start.7 = ((f32[2,32,256]{2,0,1:T(2,128)}), f32[2,32,256]{2,0,1:T(2,128)S(1)}, u32[]{:S(2)}, u32[]{:S(2)}) async-start(f32[2,32,256]{2,0,1:T(2,128)} %copy.182), calls=%async_computation.7 | async-start | bytes 131072 | tf_op jit(solution)/shard_map/all_to_all | solution.py:122
  (20 other events, 54.6 us)
Sparse Core Ops, SparseCore 0:
  132.7 131.2 all-reduce.3
where the time goes:
time: 278 us; the launch traced here: 277 us
  waiting for transfers between devices  109 us (39%)
  starting transfers between devices  45.2 us (16%)
  blocking collectives  40 us (14%)
  local copies, waits for them, and re-layouts  32.6 us (12%)
  other arithmetic  17.3 us (6%)
  matrix products  17.3 us (6%)
  between operations  15 us (5%)
    psum x1, waiting for transfers between devices, body(): summed = lax.psum(totals, ('tile', 'depth'))  84 us
    psum x1, blocking collectives, body(): summed = lax.psum(totals, ('tile', 'depth'))  40 us
    all_to_all x4, starting transfers between devices, to_columns(): lax.all_to_all(segment, 'depth', split_axis=2, concat_axis=1, tiled=True)  16.1 us
    all_to_all x4, starting transfers between devices, to_segments(): lax.all_to_all(shaped, 'depth', split_axis=1, concat_axis=2, tiled=True)  15.6 us
    all_to_all x4, waiting for transfers between devices, to_segments(): lax.all_to_all(shaped, 'depth', split_axis=1, concat_axis=2, tiled=True)  13.8 us
    unnamed x64, local copies, waits for them, and re-layouts  10.7 us
    all_to_all x4, waiting for transfers between devices, to_columns(): lax.all_to_all(segment, 'depth', split_axis=2, concat_axis=1, tiled=True)  9.74 us
    ppermute x5, starting transfers between devices, with_halo(): lax.ppermute(head, axis, [((i + 1) % count, i) for i in range(count)])  6.25 us
  transfers between devices with their start and end apart: 24, of which 8 were waited for; matrix products, arithmetic and copies ran while one was open for 11% of the time, Pallas kernels for 0%

commit v1 on v0

--- a/solution.py
+++ b/solution.py
@@ -114,7 +114,12 @@
     weight_sums = neighbour_sum(weight[None, :])[0]
 
     def to_columns(segment):
-        full_cols = lax.all_to_all(segment, "depth", split_axis=2, concat_axis=1, tiled=True)
+        full_cols = jnp.concatenate(
+            lax.all_to_all(
+                jnp.stack(jnp.split(segment, lax.axis_size("depth"), axis=2)), "depth", 0, 0
+            ),
+            axis=1,
+        )
         return full_cols.reshape(FEATURES, full_cols.shape[2])
 
     def to_segments(values):

time: 278 us -> 289 us (1.040)
  other arithmetic: 17.3 us -> 25.4 us
    unnamed x64 -> x66, local copies, waits for them, and re-layouts: 10.7 us -> 1.08 us
    all_to_all x4, waiting for transfers between devices: 9.74 us -> 5.64 us  [to_columns(): lax.all_to_all(jnp.stack(jnp.split(segment, lax.axis_size('depth'), axis=...]
    psum x1, waiting for transfers between devices: 84 us -> 87.2 us  [body(): summed = lax.psum(totals, ('tile', 'depth'))]
  transfers between devices with their start and end apart: 24 -> 24, of which waited for: 8 -> 7; matrix products, arithmetic and copies ran while one was open for 11% -> 14% of each run, Pallas kernels for 0% -> 0%
where the time goes in v1:
time: 289 us; the launch traced here: 287 us
  waiting for transfers between devices  108 us (37%)
  starting transfers between devices  46.8 us (16%)
  blocking collectives  40.2 us (14%)
  local copies, waits for them, and re-layouts  34.9 us (12%)
  other arithmetic  25.4 us (9%)
  matrix products  17.1 us (6%)
  between operations  14.8 us (5%)
    psum x1, waiting for transfers between devices, body(): summed = lax.psum(totals, ('tile', 'depth'))  87.2 us
    psum x1, blocking collectives, body(): summed = lax.psum(totals, ('tile', 'depth'))  40.2 us
    all_to_all x4, starting transfers between devices, to_segments(): lax.all_to_all(shaped, 'depth', split_axis=1, concat_axis=2, tiled=True)  17.7 us
    all_to_all x4, starting transfers between devices, to_columns(): lax.all_to_all(jnp.stack(jnp.split(segment, lax.axis_size('depth'), axis=...  15.4 us
    all_to_all x4, waiting for transfers between devices, to_segments(): lax.all_to_all(shaped, 'depth', split_axis=1, concat_axis=2, tiled=True)  13.3 us
    ppermute x5, starting transfers between devices, with_halo(): lax.ppermute(head, axis, [((i + 1) % count, i) for i in range(count)])  6.2 us
    add x5, other arithmetic, neighbour_sum(): west_cells + east_cells + south_cells + north_cells  6.08 us
  transfers between devices with their start and end apart: 24, of which 7 were waited for; matrix products, arithmetic and copies ran while one was open for 14% of the time, Pallas kernels for 0%

profile of v1, /device:TPU:0, one launch (start us, length us, event | category | flops | bytes accessed | tf_op | source)
XLA Modules:
  0.0 286.9 jit_solution(528740277648934418)
XLA Ops:
  8.2 3.4 %collective-permute-start.4 = (f32[1,1,2,32]{3,2,1,0:T(2,128)S(1)}, f32[1,1,2,32]{3,2,1,0:T(2,128)S(1)}, u32[]{:S(2)}, u32[]{:S(2)}) collective-permute-start(f32[1,1,2,32]{3,2,1,0:T(2,128)S(1)} %maximum_bitcast_fusion.4), channel_id=1, source_target_pairs={{4,0},{8,4},{12,8},{16,12},{20,16},{24,20},{28,24},{0,28},{5,1},{9... | collective-permute-start | bytes 776 | tf_op jit(solution)/shard_map/ppermute | solution.py:24
  13.0 2.7 collective-permute-start.1
  17.8 5.0 %all-to-all-start = ((bf16[4,2,8,256]{3,2,1,0:T(8,128)(2,1)}), bf16[4,2,8,256]{3,2,1,0:T(8,128)(2,1)S(1)}, u32[]{:S(2)}, u32[]{:S(2)}) async-start(bf16[4,2,8,256]{3,2,1,0:T(8,128)(2,1)} %pad_maximum_fusion), calls=%async_computation | async-start | bytes 65536 | tf_op jit(solution)/shard_map/all_to_all | solution.py:118
  26.5 1.7 collective-permute-done.2
  32.9 5.1 %all-to-all-start.1 = ((f32[2,32,256]{2,0,1:T(2,128)}), f32[2,32,256]{2,0,1:T(2,128)}, u32[]{:S(2)}, u32[]{:S(2)}) async-start(f32[2,32,256]{2,0,1:T(2,128)} %copy.117), calls=%async_computation.1 | async-start | bytes 131072 | tf_op jit(solution)/shard_map/all_to_all | solution.py:127
  39.3 4.5 %all-to-all-done.1 = f32[2,32,256]{2,0,1:T(2,128)} async-done(((f32[2,32,256]{2,0,1:T(2,128)}), f32[2,32,256]{2,0,1:T(2,128)}, u32[]{:S(2)}, u32[]{:S(2)}) %all-to-all-start.1) | async-done | bytes 65568 | tf_op jit(solution)/shard_map/all_to_all | solution.py:127
  46.8 1.6 collective-permute-start.8
  49.0 3.3 %all-to-all-start.2 = ((bf16[4,2,8,256]{3,2,1,0:T(8,128)(2,1)}), bf16[4,2,8,256]{3,2,1,0:T(8,128)(2,1)S(1)}, u32[]{:S(2)}, u32[]{:S(2)}) async-start(bf16[4,2,8,256]{3,2,1,0:T(8,128)(2,1)} %pad_maximum_fusion.1), calls=%async_computation.2 | async-start | bytes 65536 | tf_op jit(solution)/shard_map/all_to_all | solution.py:118
  54.2 3.8 %all-to-all-done.2 = bf16[4,2,8,256]{3,2,1,0:T(8,128)(2,1)S(1)} async-done(((bf16[4,2,8,256]{3,2,1,0:T(8,128)(2,1)}), bf16[4,2,8,256]{3,2,1,0:T(8,128)(2,1)S(1)}, u32[]{:S(2)}, u32[]{:S(2)}) %all-to-all-start.2) | async-done | bytes 32800 | tf_op jit(solution)/shard_map/all_to_all | solution.py:118
  61.1 3.9 %all-to-all-start.3 = ((f32[2,32,256]{2,0,1:T(2,128)}), f32[2,32,256]{2,0,1:T(2,128)}, u32[]{:S(2)}, u32[]{:S(2)}) async-start(f32[2,32,256]{2,0,1:T(2,128)} %copy.122), calls=%async_computation.3 | async-start | bytes 131072 | tf_op jit(solution)/shard_map/all_to_all | solution.py:127
  66.5 4.4 %all-to-all-done.3 = f32[2,32,256]{2,0,1:T(2,128)} async-done(((f32[2,32,256]{2,0,1:T(2,128)}), f32[2,32,256]{2,0,1:T(2,128)}, u32[]{:S(2)}, u32[]{:S(2)}) %all-to-all-start.3) | async-done | bytes 65568 | tf_op jit(solution)/shard_map/all_to_all | solution.py:127
  76.5 3.9 %all-to-all-start.4 = ((bf16[4,2,8,256]{3,2,1,0:T(8,128)(2,1)}), bf16[4,2,8,256]{3,2,1,0:T(8,128)(2,1)}, u32[]{:S(2)}, u32[]{:S(2)}) async-start(bf16[4,2,8,256]{3,2,1,0:T(8,128)(2,1)} %pad_maximum_fusion.2), calls=%async_computation.4 | async-start | bytes 65536 | tf_op jit(solution)/shard_map/all_to_all | solution.py:118
  84.3 1.8 all-to-all-done.4
  87.7 2.2 convert_reduce_fusion.1
  93.3 3.9 %all-to-all-start.5 = ((f32[2,32,256]{2,0,1:T(2,128)}), f32[2,32,256]{2,0,1:T(2,128)}, u32[]{:S(2)}, u32[]{:S(2)}) async-start(f32[2,32,256]{2,0,1:T(2,128)} %copy.127), calls=%async_computation.5 | async-start | bytes 131072 | tf_op jit(solution)/shard_map/all_to_all | solution.py:127
  98.6 4.4 %all-to-all-done.5 = f32[2,32,256]{2,0,1:T(2,128)} async-done(((f32[2,32,256]{2,0,1:T(2,128)}), f32[2,32,256]{2,0,1:T(2,128)}, u32[]{:S(2)}, u32[]{:S(2)}) %all-to-all-start.5) | async-done | bytes 65568 | tf_op jit(solution)/shard_map/all_to_all | solution.py:127
  103.9 1.5 multiply_convert_fusion.4
  105.4 1.7 reshape.235
  114.0 3.3 %all-to-all-start.6 = ((bf16[4,2,8,256]{3,2,1,0:T(8,128)(2,1)}), bf16[4,2,8,256]{3,2,1,0:T(8,128)(2,1)S(1)}, u32[]{:S(2)}, u32[]{:S(2)}) async-start(bf16[4,2,8,256]{3,2,1,0:T(8,128)(2,1)} %pad_maximum_fusion.3), calls=%async_computation.6 | async-start | bytes 65536 | tf_op jit(solution)/shard_map/all_to_all | solution.py:118
  123.0 1.6 copy.129
  125.9 1.6 copy.130
  127.4 2.3 fusion.19
  129.7 1.7 add.304
  131.4 1.8 convolution_add_fusion.5
  133.2 2.1 convert_reduce_fusion
  136.4 1.7 convolution_add_fusion
  140.1 4.8 %all-to-all-start.7 = ((f32[2,32,256]{2,0,1:T(2,128)}), f32[2,32,256]{2,0,1:T(2,128)S(1)}, u32[]{:S(2)}, u32[]{:S(2)}) async-start(f32[2,32,256]{2,0,1:T(2,128)} %copy.132), calls=%async_computation.7 | async-start | bytes 131072 | tf_op jit(solution)/shard_map/all_to_all | solution.py:127
  145.0 40.2 %all-reduce = (f32[640]{0:T(1024)S(1)}, f32[640]{0:T(1024)S(1)}, f32[64]{0:T(128)S(1)}) all-reduce(f32[640]{0:T(1024)S(1)} %add.310, f32[640]{0:T(1024)S(1)} %add.312, f32[64]{0:T(128)S(1)} %add.315), channel_id=1, replica_groups=mesh['tile'=8,'depth'=4] {'tile','depth'}, use_global_device_ids=true, to_apply=%region_3.4 | all-reduce | flops 1344 | bytes 10752 | tf_op jit(solution)/shard_map/psum | solution.py:155
  187.0 87.2 %all-reduce.4.cloned.1.call-done = (f32[64,640]{1,0:T(8,128)}, f32[640,640]{1,0:T(8,128)}, f32[640,64]{0,1:T(8,128)}) async-done(((f32[64,640]{1,0:T(8,128)}, f32[640,640]{1,0:T(8,128)}, f32[640,64]{0,1:T(8,128)}), (f32[64,640]{1,0:T(8,128)}, f32[640,640]{1,0:T(8,128)}, f32[640,64]{0,1:T(8,128)})) %all-reduce.4.cloned.1.call-update) | async-done | bytes 1966096 | tf_op jit(solution)/shard_map/psum | solution.py:155
  274.2 1.6 broadcast_multiply_fusion.6
  275.8 1.6 broadcast_multiply_fusion.5
  277.4 2.7 broadcast_multiply_fusion
  (226 shorter events, 59.4 us)
Async XLA Ops:
  7.2 23.5 %copy-start = (bf16[640,640]{1,0:T(8,128)(2,1)S(1)}, bf16[640,640]{1,0:T(8,128)(2,1)}, u32[]{:S(2)}) copy-start(bf16[640,640]{1,0:T(8,128)(2,1)} %param.16) | copy-start | bytes 2457604
  8.0 95.9 %copy-start.16 = (f32[1024]{0:T(1024)}, f32[1024]{0:T(1024)S(1)}, u32[]{:S(2)}) copy-start(f32[1024]{0:T(1024)S(1)} %get-tuple-element.85) | copy-start | bytes 12292
  8.2 18.0 %collective-permute-start.4 = (f32[1,1,2,32]{3,2,1,0:T(2,128)S(1)}, f32[1,1,2,32]{3,2,1,0:T(2,128)S(1)}, u32[]{:S(2)}, u32[]{:S(2)}) collective-permute-start(f32[1,1,2,32]{3,2,1,0:T(2,128)S(1)} %maximum_bitcast_fusion.4), channel_id=1, source_target_pairs={{4,0},{8,4},{12,8},{16,12},{20,16},{24,20},{28,24},{0,28},{5,1},{9... | collective-permute-start | bytes 776 | tf_op jit(solution)/shard_map/ppermute | solution.py:24
  11.6 12.8 %collective-permute-start.3 = (f32[1,1,2,32]{3,2,1,0:T(2,128)S(1)}, f32[1,1,2,32]{3,2,1,0:T(2,128)S(1)}, u32[]{:S(2)}, u32[]{:S(2)}) collective-permute-start(f32[1,1,2,32]{3,2,1,0:T(2,128)S(1)} %maximum_bitcast_fusion.4), channel_id=1, source_target_pairs={{0,4},{4,8},{8,12},{12,16},{16,20},{20,24},{24,28},{28,0},{1,5},{5... | collective-permute-start | bytes 776 | tf_op jit(solution)/shard_map/ppermute | solution.py:22
  13.0 15.1 %collective-permute-start.1 = (f32[1,16,2,32]{3,1,2,0:T(8,128)S(1)}, f32[1,16,2,32]{3,1,2,0:T(8,128)S(1)}, u32[]{:S(2)}, u32[]{:S(2)}) collective-permute-start(f32[1,16,2,32]{3,1,2,0:T(8,128)S(1)} %maximum_bitcast_fusion), channel_id=1, source_target_pairs={{4,0},{8,4},{12,8},{16,12},{20,16},{24,20},{28,24},{0,28},{5,1},{9... | collective-permute-start | bytes 12296 | tf_op jit(solution)/shard_map/ppermute | solution.py:24
  15.7 12.5 %collective-permute-start = (f32[1,16,2,32]{3,1,2,0:T(8,128)S(1)}, f32[1,16,2,32]{3,1,2,0:T(8,128)S(1)}, u32[]{:S(2)}, u32[]{:S(2)}) collective-permute-start(f32[1,16,2,32]{3,1,2,0:T(8,128)S(1)} %maximum_bitcast_fusion), channel_id=1, source_target_pairs={{0,4},{4,8},{8,12},{12,16},{16,20},{20,24},{24,28},{28,0},{1,5},{5... | collective-permute-start | bytes 12296 | tf_op jit(solution)/shard_map/ppermute | solution.py:22
  15.8 10.2 %collective-permute-start.5 = (f32[1,2,32]{2,1,0:T(2,128)S(1)}, f32[1,2,32]{2,1,0:T(2,128)S(1)}, u32[]{:S(2)}, u32[]{:S(2)}) collective-permute-start(f32[1,2,32]{2,1,0:T(2,128)S(1)} %pad_maximum_fusion.8), channel_id=1, source_target_pairs={{0,16},{4,20},{8,24},{12,28},{16,0},{20,4},{24,8},{28,12},{1,17},{... | collective-permute-start | bytes 776 | tf_op jit(solution)/shard_map/ppermute | solution.py:33
  17.8 12.2 %all-to-all-start = ((bf16[4,2,8,256]{3,2,1,0:T(8,128)(2,1)}), bf16[4,2,8,256]{3,2,1,0:T(8,128)(2,1)S(1)}, u32[]{:S(2)}, u32[]{:S(2)}) async-start(bf16[4,2,8,256]{3,2,1,0:T(8,128)(2,1)} %pad_maximum_fusion), calls=%async_computation | async-start | bytes 65536 | tf_op jit(solution)/shard_map/all_to_all | solution.py:118
  24.4 3.7 %collective-permute-start.2 = (f32[16,2,32]{2,1,0:T(2,128)S(1)}, f32[16,2,32]{2,1,0:T(2,128)S(1)}, u32[]{:S(2)}, u32[]{:S(2)}) collective-permute-start(f32[16,2,32]{2,1,0:T(2,128)S(1)} %pad_maximum_fusion.4), channel_id=1, source_target_pairs={{0,16},{4,20},{8,24},{12,28},{16,0},{20,4},{24,8},{28,12},{1,17},{... | collective-permute-start | bytes 12296 | tf_op jit(solution)/shard_map/ppermute | solution.py:33
  26.5 77.4 %copy-start.19 = (f32[1024]{0:T(1024)}, f32[1024]{0:T(1024)S(1)}, u32[]{:S(2)}) copy-start(f32[1024]{0:T(1024)S(1)} %add.265) | copy-start | bytes 12292
  32.9 10.9 %all-to-all-start.1 = ((f32[2,32,256]{2,0,1:T(2,128)}), f32[2,32,256]{2,0,1:T(2,128)}, u32[]{:S(2)}, u32[]{:S(2)}) async-start(f32[2,32,256]{2,0,1:T(2,128)} %copy.117), calls=%async_computation.1 | async-start | bytes 131072 | tf_op jit(solution)/shard_map/all_to_all | solution.py:127
  45.2 7.1 %collective-permute-start.7 = (f32[1,16,2,32]{3,1,2,0:T(8,128)S(1)}, f32[1,16,2,32]{3,1,2,0:T(8,128)S(1)}, u32[]{:S(2)}, u32[]{:S(2)}) collective-permute-start(f32[1,16,2,32]{3,1,2,0:T(8,128)S(1)} %maximum_bitcast_fusion.1), channel_id=1, source_target_pairs={{4,0},{8,4},{12,8},{16,12},{20,16},{24,20},{28,24},{0,28},{5,1},{9... | collective-permute-start | bytes 12296 | tf_op jit(solution)/shard_map/ppermute | solution.py:24
  45.3 7.1 %collective-permute-start.6 = (f32[1,16,2,32]{3,1,2,0:T(8,128)S(1)}, f32[1,16,2,32]{3,1,2,0:T(8,128)S(1)}, u32[]{:S(2)}, u32[]{:S(2)}) collective-permute-start(f32[1,16,2,32]{3,1,2,0:T(8,128)S(1)} %maximum_bitcast_fusion.1), channel_id=1, source_target_pairs={{0,4},{4,8},{8,12},{12,16},{16,20},{20,24},{24,28},{28,0},{1,5},{5... | collective-permute-start | bytes 12296 | tf_op jit(solution)/shard_map/ppermute | solution.py:22
  45.9 12.9 %copy-start.32 = (f32[640]{0:T(1024)S(1)}, f32[640]{0:T(1024)}, u32[]{:S(2)}) copy-start(f32[640]{0:T(1024)} %param.17) | copy-start | bytes 7684
  46.8 5.5 %collective-permute-start.8 = (f32[16,2,32]{2,1,0:T(2,128)S(1)}, f32[16,2,32]{2,1,0:T(2,128)S(1)}, u32[]{:S(2)}, u32[]{:S(2)}) collective-permute-start(f32[16,2,32]{2,1,0:T(2,128)S(1)} %pad_maximum_fusion.5), channel_id=1, source_target_pairs={{0,16},{4,20},{8,24},{12,28},{16,0},{20,4},{24,8},{28,12},{1,17},{... | collective-permute-start | bytes 12296 | tf_op jit(solution)/shard_map/ppermute | solution.py:33
  49.0 8.9 %all-to-all-start.2 = ((bf16[4,2,8,256]{3,2,1,0:T(8,128)(2,1)}), bf16[4,2,8,256]{3,2,1,0:T(8,128)(2,1)S(1)}, u32[]{:S(2)}, u32[]{:S(2)}) async-start(bf16[4,2,8,256]{3,2,1,0:T(8,128)(2,1)} %pad_maximum_fusion.1), calls=%async_computation.2 | async-start | bytes 65536 | tf_op jit(solution)/shard_map/all_to_all | solution.py:118
  61.1 9.7 %all-to-all-start.3 = ((f32[2,32,256]{2,0,1:T(2,128)}), f32[2,32,256]{2,0,1:T(2,128)}, u32[]{:S(2)}, u32[]{:S(2)}) async-start(f32[2,32,256]{2,0,1:T(2,128)} %copy.122), calls=%async_computation.3 | async-start | bytes 131072 | tf_op jit(solution)/shard_map/all_to_all | solution.py:127
  73.7 8.3 %collective-permute-start.10 = (f32[1,16,2,32]{3,1,2,0:T(8,128)S(1)}, f32[1,16,2,32]{3,1,2,0:T(8,128)S(1)}, u32[]{:S(2)}, u32[]{:S(2)}) collective-permute-start(f32[1,16,2,32]{3,1,2,0:T(8,128)S(1)} %maximum_bitcast_fusion.2), channel_id=1, source_target_pairs={{4,0},{8,4},{12,8},{16,12},{20,16},{24,20},{28,24},{0,28},{5,1},{9... | collective-permute-start | bytes 12296 | tf_op jit(solution)/shard_map/ppermute | solution.py:24
  73.8 6.6 %collective-permute-start.9 = (f32[1,16,2,32]{3,1,2,0:T(8,128)S(1)}, f32[1,16,2,32]{3,1,2,0:T(8,128)S(1)}, u32[]{:S(2)}, u32[]{:S(2)}) collective-permute-start(f32[1,16,2,32]{3,1,2,0:T(8,128)S(1)} %maximum_bitcast_fusion.2), channel_id=1, source_target_pairs={{0,4},{4,8},{8,12},{12,16},{16,20},{20,24},{24,28},{28,0},{1,5},{5... | collective-permute-start | bytes 12296 | tf_op jit(solution)/shard_map/ppermute | solution.py:22
  75.3 5.1 %collective-permute-start.11 = (f32[16,2,32]{2,1,0:T(2,128)S(1)}, f32[16,2,32]{2,1,0:T(2,128)S(1)}, u32[]{:S(2)}, u32[]{:S(2)}) collective-permute-start(f32[16,2,32]{2,1,0:T(2,128)S(1)} %pad_maximum_fusion.6), channel_id=1, source_target_pairs={{0,16},{4,20},{8,24},{12,28},{16,0},{20,4},{24,8},{28,12},{1,17},{... | collective-permute-start | bytes 12296 | tf_op jit(solution)/shard_map/ppermute | solution.py:33
  76.5 9.6 %all-to-all-start.4 = ((bf16[4,2,8,256]{3,2,1,0:T(8,128)(2,1)}), bf16[4,2,8,256]{3,2,1,0:T(8,128)(2,1)}, u32[]{:S(2)}, u32[]{:S(2)}) async-start(bf16[4,2,8,256]{3,2,1,0:T(8,128)(2,1)} %pad_maximum_fusion.2), calls=%async_computation.4 | async-start | bytes 65536 | tf_op jit(solution)/shard_map/all_to_all | solution.py:118
  93.3 9.7 %all-to-all-start.5 = ((f32[2,32,256]{2,0,1:T(2,128)}), f32[2,32,256]{2,0,1:T(2,128)}, u32[]{:S(2)}, u32[]{:S(2)}) async-start(f32[2,32,256]{2,0,1:T(2,128)} %copy.127), calls=%async_computation.5 | async-start | bytes 131072 | tf_op jit(solution)/shard_map/all_to_all | solution.py:127
  109.0 15.6 %collective-permute-start.13 = (f32[1,16,2,32]{3,1,2,0:T(8,128)}, f32[1,16,2,32]{3,1,2,0:T(8,128)}, u32[]{:S(2)}, u32[]{:S(2)}) collective-permute-start(f32[1,16,2,32]{3,1,2,0:T(8,128)} %maximum_bitcast_fusion.3), channel_id=1, source_target_pairs={{4,0},{8,4},{12,8},{16,12},{20,16},{24,20},{28,24},{0,28},{5,1},{9... | collective-permute-start | bytes 12296 | tf_op jit(solution)/shard_map/ppermute | solution.py:24
  109.0 9.9 %collective-permute-start.12 = (f32[1,16,2,32]{3,1,2,0:T(8,128)}, f32[1,16,2,32]{3,1,2,0:T(8,128)}, u32[]{:S(2)}, u32[]{:S(2)}) collective-permute-start(f32[1,16,2,32]{3,1,2,0:T(8,128)} %maximum_bitcast_fusion.3), channel_id=1, source_target_pairs={{0,4},{4,8},{8,12},{12,16},{16,20},{20,24},{24,28},{28,0},{1,5},{5... | collective-permute-start | bytes 12296 | tf_op jit(solution)/shard_map/ppermute | solution.py:22
  111.9 5.6 %collective-permute-start.14 = (f32[16,2,32]{2,1,0:T(2,128)}, f32[16,2,32]{2,1,0:T(2,128)}, u32[]{:S(2)}, u32[]{:S(2)}) collective-permute-start(f32[16,2,32]{2,1,0:T(2,128)} %pad_maximum_fusion.7), channel_id=1, source_target_pairs={{0,16},{4,20},{8,24},{12,28},{16,0},{20,4},{24,8},{28,12},{1,17},{... | collective-permute-start | bytes 12296 | tf_op jit(solution)/shard_map/ppermute | solution.py:33
  114.0 17.4 %all-to-all-start.6 = ((bf16[4,2,8,256]{3,2,1,0:T(8,128)(2,1)}), bf16[4,2,8,256]{3,2,1,0:T(8,128)(2,1)S(1)}, u32[]{:S(2)}, u32[]{:S(2)}) async-start(bf16[4,2,8,256]{3,2,1,0:T(8,128)(2,1)} %pad_maximum_fusion.3), calls=%async_computation.6 | async-start | bytes 65536 | tf_op jit(solution)/shard_map/all_to_all | solution.py:118
  117.2 156.9 %all-reduce.4.cloned.1.call-start = ((), (), s32[]{:S(2)}) async-start(), calls=%async_computation.8 | async-start | bytes 3932160 | tf_op jit(solution)/shard_map/psum | solution.py:155
  139.0 47.3 %copy-start.8 = (f32[2,8,1024]{2,1,0:T(8,128)S(1)}, f32[2,8,1024]{2,1,0:T(8,128)}, u32[]{:S(2)}) copy-start(f32[2,8,1024]{2,1,0:T(8,128)} %get-tuple-element.25) | copy-start | bytes 196612
  139.0 47.3 %copy-start.15 = (f32[2,8,1024]{2,1,0:T(8,128)S(1)}, f32[2,8,1024]{2,1,0:T(8,128)}, u32[]{:S(2)}) copy-start(f32[2,8,1024]{2,1,0:T(8,128)} %add.304) | copy-start | bytes 196612
  139.0 47.3 %copy-start.17 = (f32[1024]{0:T(1024)S(1)}, f32[1024]{0:T(1024)}, u32[]{:S(2)}) copy-start(f32[1024]{0:T(1024)} %copy-done.16) | copy-start | bytes 12292
  139.0 47.3 %copy-start.20 = (f32[1024]{0:T(1024)S(1)}, f32[1024]{0:T(1024)}, u32[]{:S(2)}) copy-start(f32[1024]{0:T(1024)} %copy-done.19) | copy-start | bytes 12292
  140.1 46.2 %all-to-all-start.7 = ((f32[2,32,256]{2,0,1:T(2,128)}), f32[2,32,256]{2,0,1:T(2,128)S(1)}, u32[]{:S(2)}, u32[]{:S(2)}) async-start(f32[2,32,256]{2,0,1:T(2,128)} %copy.132), calls=%async_computation.7 | async-start | bytes 131072 | tf_op jit(solution)/shard_map/all_to_all | solution.py:127
  (25 other events, 119.1 us)
Sparse Core Ops, SparseCore 0:
  139.2 134.9 all-reduce.3
